TPU v7x, 768 devices: a whole 4x8x12 slice. The times are simulated.
768 devices in a mesh: dp: 16 (over x, z_hi, core), fsdp: 48 (over z_lo, y).
Axes of the slice: x: 4, y: 8, z: 12 (z_hi: 2, z_lo: 6; z = z_hi * 6 + z_lo), core: 2. Of those that a mesh axis runs over, the one named last changes fastest.
Arguments:
- activations: bfloat16 [98304, 8192], P(('dp', 'fsdp')), may hold values from -6 to 6
- queries: bfloat16 [98304, 4096], P(('dp', 'fsdp')), may hold values from -5 to 5
- key_states: bfloat16 [98304, 512], P(('dp', 'fsdp')), may hold values from -5 to 5
- out_grads: bfloat16 [98304, 4096], P(('dp', 'fsdp')), may hold values from -6 to 6
- projector: bfloat16 [8192, 512], P('dp'), may hold values from -0.0625 to 0.0625
- lengths: int32 [16, 96], P('dp'), may hold values from 1 to 128, 6144 in all within a row
Outputs:
- value_grads: bfloat16 [98304, 512], P(('dp', 'fsdp'))
- gradient: float32 [512, 512], P('dp')
All inputs are finite; a program needn't handle non-finite values.
Results may differ from a plain program's by a relative error of at most 0.0048.
Values may be sent and summed in bfloat16 or wider, within the bound.
A program may use at most 64 MiB of HBM per device.

v0:
```python
import math

import jax
import jax.numpy as jnp
from jax import lax
from jax.sharding import PartitionSpec as P

HEADS = 32
KV = 4
HD = 128


def from_behind(block, axis, distance):
    devices = range(lax.axis_size(axis))
    route = [(i - distance, i) for i in devices if i - distance in devices]
    return lax.ppermute(block, axis, route)


def split_up(value, dim, length):
    before, after = (value.shape[:dim], value.shape[dim + 1 :])
    return jnp.moveaxis(value.reshape(*before, length, -1, *after), dim, 0)


def summed_on_arrival(value, axis, dim):
    pieces = split_up(value, dim, lax.axis_size(axis))
    arrived = lax.all_to_all(pieces, axis, split_axis=0, concat_axis=0, tiled=True)
    return arrived.sum(axis=0)


def from_everyone(value, axis):
    copies = jnp.broadcast_to(value, (lax.axis_size(axis), *value.shape))
    return lax.all_to_all(copies, axis, split_axis=0, concat_axis=0, tiled=True)


def of_everyone(value, axis):
    return from_everyone(value, axis).sum(axis=0)


def doc_index(positions, doc_ends):
    return jnp.sum((doc_ends[None, :] <= positions[:, None]).astype(jnp.int32), axis=1)


def local(activations, queries, key_states, out_grads, projector, lengths):
    tok_rows = queries.shape[0]
    within = lax.axis_index("fsdp")
    doc_ends = jnp.cumsum(lengths[0])
    own_pos = within * tok_rows + jnp.arange(tok_rows, dtype=jnp.int32)
    key_pos = jnp.concatenate([own_pos - tok_rows, own_pos])
    visible = doc_index(own_pos, doc_ends)[:, None] == doc_index(key_pos, doc_ends)[None, :]
    visible = visible & (key_pos[None, :] <= own_pos[:, None]) & (key_pos[None, :] >= 0)
    earlier_keys = from_behind(key_states, "fsdp", 1)
    keys_both = jnp.concatenate([earlier_keys, key_states], axis=0)
    query_heads = queries.reshape(tok_rows, KV, HEADS // KV, HD)
    key_heads = keys_both.reshape(2 * tok_rows, KV, HD)
    scores = jnp.einsum(
        "tkgd,skd->kgts", query_heads, key_heads, preferred_element_type=jnp.float32
    )
    scores = scores * (1.0 / math.sqrt(HD))
    scores = jnp.where(visible[None, None], scores, -jnp.inf)
    exponent = jnp.exp(scores - jnp.max(scores, axis=3, keepdims=True))
    weights = (exponent / jnp.sum(exponent, axis=3, keepdims=True)).astype(jnp.bfloat16)
    grad_heads = out_grads.reshape(tok_rows, KV, HEADS // KV, HD)
    value_terms = jnp.einsum(
        "kgts,tkgd->skd", weights, grad_heads, preferred_element_type=jnp.float32
    )
    value_terms = value_terms.reshape(2 * tok_rows, KV * HD)
    from_next = from_behind(value_terms[:tok_rows], "fsdp", -1)
    value_grads = (value_terms[tok_rows:] + from_next).astype(jnp.bfloat16)
    contract_rows = (((0,), (0,)), ((), ()))
    projected = jnp.dot(
        activations,
        lax.all_gather(projector, "dp", axis=0, tiled=True),
        preferred_element_type=jnp.float32,
    )
    local_term = lax.dot_general(
        projected, value_grads.astype(jnp.float32), contract_rows, precision=lax.Precision.HIGHEST
    )
    local_term = local_term * (
        1.0 / math.sqrt(tok_rows * lax.axis_size("dp") * lax.axis_size("fsdp"))
    )
    row_part = summed_on_arrival(local_term, "dp", 0)
    gradient = of_everyone(row_part, "fsdp")
    return (value_grads, gradient)


def solution(mesh):
    in_specs = (
        P(("dp", "fsdp"), None),
        P(("dp", "fsdp"), None),
        P(("dp", "fsdp"), None),
        P(("dp", "fsdp"), None),
        P("dp", None),
        P("dp", None),
    )
    out_specs = (P(("dp", "fsdp"), None), P("dp", None))
    return jax.shard_map(local, mesh=mesh, in_specs=in_specs, out_specs=out_specs, check_vma=False)
```

profile of v0, /device:TPU:1, one launch (start us, length us, event | category | flops | bytes accessed | tf_op | source)
XLA Modules:
  0.0 340.6 jit_solution(11586042916054163030)
XLA Ops:
  7.2 0.7 all-gather.2.cloned.1.call-update
  7.9 1.0 copy.24
  8.9 4.0 %collective-permute-start = (bf16[128,512]{0,1:T(8,128)(2,1)S(1)}, bf16[128,512]{0,1:T(8,128)(2,1)S(1)}, u32[]{:S(2)}, u32[]{:S(2)}) collective-permute-start(bf16[128,512]{0,1:T(8,128)(2,1)S(1)} %copy.24), channel_id=1, source_target_pairs={{0,1},{1,2},{2,3},{3,4},{4,5},{5,6},{6,7},{7,8},{8,9},{9,10},{10,1... | collective-permute-start | bytes 393224 | tf_op jit(solution)/shard_map/ppermute | solution.py:16
  13.0 0.8 copy.23
  13.7 0.1 reduce-window.8
  13.9 0.1 reduce
  14.0 1.5 copy.38
  15.4 2.3 copy.37
  18.0 0.2 and_and_fusion
  18.2 0.8 fusion.7
  19.0 1.1 fusion.12
  20.1 0.1 copy-done.1
  20.2 0.8 fusion.6
  21.1 0.1 copy.30
  21.3 1.3 collective-permute-start.1
  22.6 0.1 copy.31
  22.7 5.7 %collective-permute-done.1 = f32[128,512]{1,0:T(8,128)S(1)} collective-permute-done((f32[128,512]{1,0:T(8,128)S(1)}, f32[128,512]{1,0:T(8,128)S(1)}, u32[]{:S(2)}, u32[]{:S(2)}) %collective-permute-start.1) | collective-permute-done | bytes 262176 | tf_op jit(solution)/shard_map/ppermute | solution.py:16
  28.4 142.5 %all-gather.2.cloned.1.call-done = bf16[8192,512]{1,0:T(8,128)(2,1)} async-done(((bf16[512,512]{1,0:T(8,128)(2,1)}), bf16[8192,512]{1,0:T(8,128)(2,1)}) %all-gather.2.cloned.1.call-update) | async-done | bytes 8388624 | tf_op jit(solution)/shard_map/all_gather | solution.py:72
  170.9 4.6 %fusion.13 = f32[128,512]{1,0:T(8,128)S(1)} fusion(bf16[128,8192]{1,0:T(8,128)(2,1)S(1)} %copy-done, bf16[8192,512]{1,0:T(8,128)(2,1)} %all-gather.2.cloned.1.call-done), kind=kOutput, calls=%fused_computation.26 | convolution fusion | flops 1073741824 | bytes 10747904 | tf_op jit(solution)/shard_map/dot_general | solution.py:70
  175.6 0.6 convolution_multiply_fusion
  176.2 37.9 %all_to_all.10 = f32[16,32,512]{2,1,0:T(8,128)S(1)} all-to-all(f32[16,32,512]{2,1,0:T(8,128)S(1)} %bitcast.35), channel_id=1, replica_groups=mesh['dp'=16,'fsdp'=48] {'dp'}, dimensions={0} | all-to-all | bytes 2097152 | tf_op jit(solution)/shard_map/all_to_all | solution.py:26
  214.2 0.4 broadcast_in_dim.12
  214.5 116.5 %all_to_all.11 = f32[48,32,512]{2,1,0:T(8,128)} all-to-all(f32[48,32,512]{2,1,0:T(8,128)S(1)} %broadcast_in_dim.12), channel_id=1, replica_groups=mesh['dp'=16,'fsdp'=48] {'fsdp'}, dimensions={0} | all-to-all | bytes 6291456 | tf_op jit(solution)/shard_map/all_to_all | solution.py:32
  331.0 2.7 reduce_sum.49
  (17 shorter events, 0.5 us)
Async XLA Ops:
  7.2 163.8 %copy-start = (bf16[128,8192]{1,0:T(8,128)(2,1)S(1)}, bf16[128,8192]{1,0:T(8,128)(2,1)}, u32[]{:S(2)}) copy-start(bf16[128,8192]{1,0:T(8,128)(2,1)} %param.6) | copy-start | bytes 6291460
  7.2 163.7 %all-gather.2.cloned.1.call-start = ((), (), s32[]{:S(2)}) async-start(), calls=%async_computation.2 | async-start | bytes 8912896 | tf_op jit(solution)/shard_map/all_gather | solution.py:72
  8.9 9.3 %collective-permute-start = (bf16[128,512]{0,1:T(8,128)(2,1)S(1)}, bf16[128,512]{0,1:T(8,128)(2,1)S(1)}, u32[]{:S(2)}, u32[]{:S(2)}) collective-permute-start(bf16[128,512]{0,1:T(8,128)(2,1)S(1)} %copy.24), channel_id=1, source_target_pairs={{0,1},{1,2},{2,3},{3,4},{4,5},{5,6},{6,7},{7,8},{8,9},{9,10},{10,1... | collective-permute-start | bytes 393224 | tf_op jit(solution)/shard_map/ppermute | solution.py:16
  19.0 1.2 copy-start.1
  21.3 7.1 %collective-permute-start.1 = (f32[128,512]{1,0:T(8,128)S(1)}, f32[128,512]{1,0:T(8,128)S(1)}, u32[]{:S(2)}, u32[]{:S(2)}) collective-permute-start(f32[128,512]{1,0:T(8,128)S(1)} %copy.30), channel_id=1, source_target_pairs={{1,0},{2,1},{3,2},{4,3},{5,4},{6,5},{7,6},{8,7},{9,8},{10,9},{11,1... | collective-permute-start | bytes 786440 | tf_op jit(solution)/shard_map/ppermute | solution.py:16
  28.4 147.2 %copy-start.2 = (bf16[128,512]{1,0:T(8,128)(2,1)}, bf16[128,512]{1,0:T(8,128)(2,1)S(1)}, u32[]{:S(2)}) copy-start(bf16[128,512]{1,0:T(8,128)(2,1)S(1)} %add_convert_fusion) | copy-start | bytes 393220
Sparse Core Ops, SparseCore 0:
  11.8 159.0 all-gather.1
where the time goes:
time: 342 us; the launch traced here: 341 us
  blocking collectives  154 us (45%)
  waiting for transfers between devices  149 us (44%)
  between operations  14.2 us (4%)
  matrix products  6.85 us (2%)
  local copies, waits for them, and re-layouts  6.38 us (2%)
  starting transfers between devices  5.36 us (2%)
  other arithmetic  4.61 us (1%)
    all_gather x1, waiting for transfers between devices, local(): lax.all_gather(projector, 'dp', axis=0, tiled=True)  143 us
    all_to_all x1, blocking collectives, from_everyone(): return lax.all_to_all(copies, axis, split_axis=0, concat_axis=0, tiled=True)  116 us
    all_to_all x1, blocking collectives, summed_on_arrival(): lax.all_to_all(pieces, axis, split_axis=0, concat_axis=0, tiled=True)  37.9 us
  transfers between devices with their start and end apart: 3, of which 2 were waited for; matrix products, arithmetic and copies ran while one was open for 3% of the time, Pallas kernels for 0%

commit v1 on v0

v1 whole, which is shorter than its diff:
```python
import functools
import math

import jax
import jax.numpy as jnp
from jax import lax
from jax.experimental import pallas as pl
from jax.experimental.pallas import tpu as pltpu
from jax.sharding import PartitionSpec as P

HEADS = 32
KV = 4
HD = 128
GROUP = HEADS // KV
MESH = pl.DeviceIdType.MESH

NX, NY, NH, NL = 4, 8, 2, 6
NZ = NH * NL
BF = jnp.bfloat16
F32 = jnp.float32


def slot_of(k, o):
    return k * 2 + o


def kernel(
    scale,
    act_hbm, q_hbm, k_hbm, og_hbm, p_hbm, len_ref,
    vg_ref, grad_ref,
    q_v, og_v, kboth, a_all, p_all, terms, prev_send, prev_recv, v_all, acc,
    lhs, core_send, core_recv, x_keep, x_send, x_recv, y_keep, y_send, y_recv,
    z_send, z_recv, g_all,
    lsem, asem_s, asem_r, ksem, xsem_s, xsem_r, ysem_s, ysem_r, zsem_s, zfsem_s, zsem_r,
    psem, vsem, csem, rxs, rxr, rys, ryr, rzs, rzr, rgs, rgr,
):
    dp = lax.axis_index("dp")
    me = lax.axis_index("fsdp")
    x, half, core = dp // 4, (dp // 2) % 2, dp % 2
    y, lo = me % NY, me // NY
    z = half * NL + lo
    par = y % 2
    qa, qb = 2 * par, 2 * par + 1
    ma, mb = 2 - 2 * par, 3 - 2 * par

    def dev(xx, yy, zz, cc):
        return ((xx * 2 + zz // NL) * 2 + cc, (zz % NL) * NY + yy)

    def x_dev(k):
        return dev((x + k) % NX, y, z, core)

    def y_dev(k):
        return dev(x, (y + k) % NY, z, core)

    def z_dev(k):
        return dev(x, y, (z + k) % NZ, core)

    mate = dev(x, y, z, 1 - core)
    has_prev, has_next = me > 0, me < NY * NL - 1

    def remote(src, dst, ssem, rsem, to):
        return pltpu.make_async_remote_copy(
            src_ref=src, dst_ref=dst, send_sem=ssem, recv_sem=rsem, device_id=to, device_id_type=MESH
        )

    def a_cols(k, o, cc):
        blk = (((x + k) % NX) * 2 + (half + o) % 2) * 2 + cc
        return pl.ds(pl.multiple_of(blk * 512, 512), 512)

    def own_rows():
        return pl.ds(0, 128)

    loads = [
        pltpu.make_async_copy(k_hbm, kboth.at[pl.ds(128, 128)], lsem.at[0]),
        pltpu.make_async_copy(q_hbm, q_v, lsem.at[1]),
        pltpu.make_async_copy(og_hbm, og_v, lsem.at[2]),
        pltpu.make_async_copy(p_hbm, p_all.at[0], lsem.at[3]),
    ]
    a_loads = [
        pltpu.make_async_copy(
            act_hbm.at[:, a_cols(s // 2, s % 2, core)], a_all.at[s, pl.ds(0, 128)], lsem.at[4 + s]
        )
        for s in range(8)
    ]
    for c in loads:
        c.start()

    barrier = pltpu.get_barrier_semaphore()
    peers = [mate]
    peers += [x_dev(k) for k in range(1, NX)]
    peers += [y_dev(k) for k in range(1, NY)]
    peers += [z_dev(k) for k in range(1, NZ)]
    for to in peers:
        pl.semaphore_signal(barrier, inc=1, device_id=to, device_id_type=MESH)
    cross_next = jnp.logical_and(y == NY - 1, lo < NL - 1)
    cross_prev = jnp.logical_and(y == 0, lo > 0)

    @pl.when(cross_next)
    def _():
        pl.semaphore_signal(barrier, inc=1, device_id=(dp, me + 1), device_id_type=MESH)

    @pl.when(cross_prev)
    def _():
        pl.semaphore_signal(barrier, inc=1, device_id=(dp, me - 1), device_id_type=MESH)

    for c in a_loads:
        c.start()

    n_docs = len_ref.shape[1]
    lens = jnp.broadcast_to(len_ref[...].astype(F32), (128, n_docs)).astype(BF)
    upto = (
        lax.broadcasted_iota(jnp.int32, (n_docs, n_docs), 1)
        <= lax.broadcasted_iota(jnp.int32, (n_docs, n_docs), 0)
    )
    ends = lax.dot_general(
        jnp.where(upto, 1.0, 0.0).astype(BF), lens, (((1,), (1,)), ((), ())), preferred_element_type=F32
    ).astype(jnp.int32)
    q_pos = me * 128 + lax.broadcasted_iota(jnp.int32, (n_docs, 128), 1)
    start = jnp.max(jnp.where(ends <= q_pos, ends, 0), axis=0, keepdims=True)
    key_pos = (me - 1) * 128 + lax.broadcasted_iota(jnp.int32, (256, 128), 0)
    qry_pos = me * 128 + lax.broadcasted_iota(jnp.int32, (256, 128), 1)
    visible = jnp.logical_and(
        jnp.logical_and(key_pos >= start, key_pos <= qry_pos), key_pos >= 0
    )
    visible2 = jnp.concatenate([visible, visible], axis=1)

    @pl.when(jnp.logical_not(has_prev))
    def _():
        kboth[pl.ds(0, 128), :] = jnp.zeros((128, KV * HD), BF)

    @pl.when(jnp.logical_not(has_next))
    def _():
        prev_recv[...] = jnp.zeros((128, KV * HD), BF)

    pl.semaphore_wait(
        barrier, len(peers) + cross_next.astype(jnp.int32) + cross_prev.astype(jnp.int32)
    )

    k_copy = remote(k_hbm, kboth.at[pl.ds(0, 128)], ksem.at[0], ksem.at[1], (dp, me + 1))

    @pl.when(has_next)
    def _():
        k_copy.start()

    def quarter(q):
        return p_hbm.at[pl.ds(pl.multiple_of(q * 128, 128), 128)]

    def p_part(s, q):
        return p_all.at[s, pl.ds(pl.multiple_of(q * 128, 128), 128)]

    def x_copy(o, m):
        q = qa if m in (0, 3, 4) else qb
        k, dst = ((1, 3), (1, 3), (-1, 1), (-1, 1), (1, 2), (-1, 2))[m]
        if m < 4:
            src = quarter(q) if o == 0 else p_part(slot_of(0, 1), q)
        else:
            src = p_part(slot_of(3 if m == 4 else 1, o), q)
        return remote(
            src, p_part(slot_of(dst, o), q), xsem_s.at[o, m], xsem_r.at[o, m], x_dev(k)
        )

    def y_copy(s, m):
        q = qb if m else qa
        return remote(
            p_part(s, q), p_part(s, q), ysem_s.at[s, m], ysem_r.at[s, m], y_dev(-1 if m else 1)
        )

    def y_wait(s):
        for m, q in ((0, ma), (1, mb)):
            remote(
                p_part(s, q), p_part(s, q), ysem_s.at[s, m], ysem_r.at[s, m], y_dev(-1 if m else 1)
            ).wait_recv()

    low_side = lo < 3
    z_away = jnp.where(low_side, 1, NZ - 1)
    z_out = jnp.where(lo == 0, NZ - 1, 1)
    z_edge = jnp.logical_or(lo == 0, lo == NL - 1)
    z_mid = jnp.logical_or(lo == 2, lo == 3)
    z_second = jnp.logical_or(lo == 1, lo == 4)

    def z_own(m):
        q = qb if m else qa
        return remote(
            quarter(q), p_part(1, q), zsem_s.at[m], zsem_r.at[m], dev(x, y, (z + z_out) % NZ, core)
        )

    def z_on(m):
        q = qb if m else qa
        return remote(
            p_part(1, q), p_part(1, q), zfsem_s.at[m], zsem_r.at[m], dev(x, y, (z + z_away) % NZ, core)
        )

    @pl.when(z_edge)
    def _():
        z_own(0).start()
        z_own(1).start()

    for m in (0, 2, 1, 3):
        x_copy(0, m).start()

    a_copies = [
        remote(
            act_hbm.at[:, a_cols(s // 2, s % 2, 1 - core)],
            a_all.at[s, pl.ds(128, 128)],
            asem_s.at[s],
            asem_r.at[s],
            mate,
        )
        for s in range(8)
    ]
    for c in a_copies:
        c.start()

    def z_step(m):
        z_copy = z_on(m)
        z_copy.wait_recv()

        @pl.when(jnp.logical_not(z_mid))
        def _():
            z_copy.start()

        for mm in ((0, 3), (1, 2))[m]:
            x_copy(1, mm).start()
        y_copy(1, m).start()

    def x_first(o):
        x_copy(o, 0).wait_recv()
        x_copy(o, 4).start()
        y_copy(slot_of(3, o), 0).start()
        x_copy(o, 2).wait_recv()
        x_copy(o, 5).start()
        y_copy(slot_of(1, o), 1).start()

    def x_second(o):
        x_copy(o, 1).wait_recv()
        y_copy(slot_of(3, o), 1).start()
        x_copy(o, 3).wait_recv()
        y_copy(slot_of(1, o), 0).start()

    def x_third(o):
        x_copy(o, 4).wait_recv()
        y_copy(slot_of(2, o), 0).start()
        x_copy(o, 5).wait_recv()
        y_copy(slot_of(2, o), 1).start()

    factor = math.log2(math.e) / math.sqrt(HD)

    def attend(g):
        keys = kboth[:, g * HD : (g + 1) * HD]
        total = jnp.zeros((256, HD), F32)
        for pair in range(GROUP // 2):
            h0 = (g * GROUP + 2 * pair) * HD
            qs = jnp.concatenate([q_v[:, h0 : h0 + HD], q_v[:, h0 + HD : h0 + 2 * HD]], axis=0)
            gs = jnp.concatenate([og_v[:, h0 : h0 + HD], og_v[:, h0 + HD : h0 + 2 * HD]], axis=0)
            s = lax.dot_general(keys, qs, (((1,), (1,)), ((), ())), preferred_element_type=F32)
            s = jnp.where(visible2, s, -jnp.inf)
            e = jnp.exp2((s - jnp.max(s, axis=0, keepdims=True)) * factor)
            w = (e * (1.0 / jnp.sum(e, axis=0, keepdims=True))).astype(BF)
            total = total + jnp.dot(w, gs, preferred_element_type=F32)
        terms[:, g * HD : (g + 1) * HD] = total[128:]
        prev_send[:, g * HD : (g + 1) * HD] = total[:128].astype(BF)

    for c in loads[:3]:
        c.wait()
    x_first(0)

    @pl.when(has_prev)
    def _():
        k_copy.wait_recv()

    attend(0)
    attend(1)

    @pl.when(z_edge)
    def _():
        z_step(0)

    x_second(0)
    attend(2)

    @pl.when(z_edge)
    def _():
        z_step(1)

    attend(3)
    prev_copy = remote(prev_send, prev_recv, psem.at[0], psem.at[1], (dp, me - 1))

    @pl.when(has_prev)
    def _():
        prev_copy.start()

    x_third(0)

    @pl.when(z_second)
    def _():
        z_step(0)
        z_step(1)

    loads[3].wait()
    for c in a_loads:
        c.wait()
    for c in a_copies:
        c.wait_recv()

    def project(s):
        return jnp.dot(a_all[s], p_all[s], preferred_element_type=F32)

    acc[...] = project(0)

    @pl.when(has_next)
    def _():
        prev_copy.wait_recv()

    grads = (terms[...] + prev_recv[...].astype(F32)).astype(BF)
    vg_ref[...] = grads
    v_all[pl.ds(0, 128), :] = grads
    v_copy = remote(
        v_all.at[pl.ds(0, 128)], v_all.at[pl.ds(128, 128)], vsem.at[0], vsem.at[1], mate
    )
    v_copy.start()

    @pl.when(z_mid)
    def _():
        z_step(0)
        z_step(1)

    x_first(1)
    y_wait(slot_of(3, 0))
    acc[...] += project(slot_of(3, 0))
    y_wait(slot_of(1, 0))
    acc[...] += project(slot_of(1, 0))
    x_second(1)
    y_wait(slot_of(2, 0))
    acc[...] += project(slot_of(2, 0))
    x_third(1)
    for k in (0, 3, 1, 2):
        y_wait(slot_of(k, 1))
        acc[...] += project(slot_of(k, 1))

    flipped = acc[...].T
    high = flipped.astype(BF)
    low = (flipped - high.astype(F32)).astype(BF)
    for b in range(16):
        rows = slice(b // 2 * 32, b // 2 * 32 + 32)
        lhs[b % 2, rows, :256] = high[b * 32 : b * 32 + 32]
        lhs[b % 2, rows, 256:] = low[b * 32 : b * 32 + 32]
    v_copy.wait_recv()
    values = jnp.concatenate([v_all[...], v_all[...]], axis=0)
    core_send[...] = (jnp.dot(lhs[1 - core], values, preferred_element_type=F32) * scale).astype(BF)
    core_copy = remote(core_send, core_recv, csem.at[0], csem.at[1], mate)
    core_copy.start()
    mine = jnp.dot(lhs[core], values, preferred_element_type=F32) * scale
    core_copy.wait_recv()
    mine = (mine + core_recv[...].astype(F32)).reshape(NX, 64, 512)
    x_keep[...] = mine
    x_send[...] = mine.astype(BF)
    rx = [
        remote(x_send.at[(x + k) % NX], x_recv.at[k - 1], rxs.at[k - 1], rxr.at[k - 1], x_dev(k))
        for k in range(1, NX)
    ]
    for k in (2, 1, 3):
        rx[k - 1].start()
    mine = x_keep[x]
    for k in (1, 3, 2):
        rx[k - 1].wait_recv()
        mine = mine + x_recv[k - 1].astype(F32)
    for yy in range(NY):
        for h in range(NH):
            r0 = h * 32 + yy // 4 * 16
            c0 = yy % 4 * 128
            piece = mine[r0 : r0 + 16, c0 : c0 + 128]
            y_keep[yy, h] = piece
            y_send[yy, h] = piece.astype(BF)
    ry = [
        remote(y_send.at[(y + k) % NY], y_recv.at[k - 1], rys.at[k - 1], ryr.at[k - 1], y_dev(k))
        for k in range(1, NY)
    ]
    for k in (4, 3, 5, 2, 6, 1, 7):
        ry[k - 1].start()
    mine = y_keep[y]
    for k in (1, 7, 2, 6, 3, 5, 4):
        ry[k - 1].wait_recv()
        mine = mine + y_recv[k - 1].astype(F32)
    z_send[...] = mine
    rz = [
        remote(
            z_send.at[((z + k) % NZ) // NL], z_recv.at[k - 1], rzs.at[k - 1], rzr.at[k - 1], z_dev(k)
        )
        for k in range(1, NZ)
    ]
    for k in (6, 5, 7, 4, 8, 3, 9, 2, 10, 1, 11):
        rz[k - 1].start()
    mine = z_send[half]
    for k in (1, 11, 2, 10, 3, 9, 4, 8, 5, 7, 6):
        rz[k - 1].wait_recv()
        mine = mine + z_recv[k - 1]
    g_all[y] = mine
    rg = [
        remote(g_all.at[y], g_all.at[y], rgs.at[k - 1], rgr.at[k - 1], y_dev(k)) for k in range(1, NY)
    ]
    for k in (4, 3, 5, 2, 6, 1, 7):
        rg[k - 1].start()
    for k in range(1, NY):
        sender = (y + NY - k) % NY
        remote(
            g_all.at[sender], g_all.at[sender], rgs.at[k - 1], rgr.at[k - 1], y_dev(k)
        ).wait_recv()
    for yy in range(NY):
        grad_ref[pl.ds(yy // 4 * 16, 16), pl.ds(yy % 4 * 128, 128)] = g_all[yy]

    @pl.when(has_next)
    def _():
        k_copy.wait_send()

    @pl.when(has_prev)
    def _():
        prev_copy.wait_send()

    @pl.when(z_edge)
    def _():
        z_own(0).wait_send()
        z_own(1).wait_send()

    @pl.when(jnp.logical_not(z_mid))
    def _():
        z_on(0).wait_send()
        z_on(1).wait_send()

    for o in range(2):
        for m in range(6):
            x_copy(o, m).wait_send()
    for s in range(1, 8):
        for m in range(2):
            y_copy(s, m).wait_send()
    for c in a_copies + [v_copy, core_copy] + rx + ry + rz + rg:
        c.wait_send()


def local(activations, queries, key_states, out_grads, projector, lengths):
    toks = queries.shape[0]
    scale = 1.0 / math.sqrt(toks * lax.axis_size("dp") * lax.axis_size("fsdp"))
    dma, vmem = pltpu.SemaphoreType.DMA, pltpu.VMEM
    any_spec = pl.BlockSpec(memory_space=pl.ANY)
    vmem_spec = pl.BlockSpec(memory_space=pltpu.VMEM)
    return pl.pallas_call(
        functools.partial(kernel, scale),
        out_shape=(
            jax.ShapeDtypeStruct((toks, KV * HD), BF),
            jax.ShapeDtypeStruct((32, KV * HD), F32),
        ),
        in_specs=[any_spec] * 5 + [vmem_spec],
        out_specs=(vmem_spec, vmem_spec),
        scratch_shapes=[
            vmem((toks, HEADS * HD), BF),
            vmem((toks, HEADS * HD), BF),
            vmem((2 * toks, KV * HD), BF),
            vmem((8, 2 * toks, 512), BF),
            vmem((8, 512, 512), BF),
            vmem((toks, KV * HD), F32),
            vmem((toks, KV * HD), BF),
            vmem((toks, KV * HD), BF),
            vmem((2 * toks, KV * HD), BF),
            vmem((2 * toks, 512), F32),
            vmem((2, 256, 512), BF),
            vmem((256, 512), BF),
            vmem((256, 512), BF),
            vmem((NX, 64, 512), F32),
            vmem((NX, 64, 512), BF),
            vmem((NX - 1, 64, 512), BF),
            vmem((NY, NH, 16, 128), F32),
            vmem((NY, NH, 16, 128), BF),
            vmem((NY - 1, NH, 16, 128), BF),
            vmem((NH, 16, 128), F32),
            vmem((NZ - 1, 16, 128), F32),
            vmem((NY, 16, 128), F32),
            dma((12,)),
            dma((8,)),
            dma((8,)),
            dma((2,)),
            dma((2, 6)),
            dma((2, 6)),
            dma((8, 2)),
            dma((8, 2)),
            dma((2,)),
            dma((2,)),
            dma((2,)),
            dma((2,)),
            dma((2,)),
            dma((2,)),
            dma((NX - 1,)),
            dma((NX - 1,)),
            dma((NY - 1,)),
            dma((NY - 1,)),
            dma((NZ - 1,)),
            dma((NZ - 1,)),
            dma((NY - 1,)),
            dma((NY - 1,)),
        ],
        compiler_params=pltpu.CompilerParams(collective_id=0, has_side_effects=True),
    )(activations, queries, key_states, out_grads, projector, lengths)


def solution(mesh):
    in_specs = (
        P(("dp", "fsdp"), None),
        P(("dp", "fsdp"), None),
        P(("dp", "fsdp"), None),
        P(("dp", "fsdp"), None),
        P("dp", None),
        P("dp", None),
    )
    out_specs = (P(("dp", "fsdp"), None), P("dp", None))
    return jax.shard_map(local, mesh=mesh, in_specs=in_specs, out_specs=out_specs, check_vma=False)
```

time: 342 us -> 78.3 us (0.23)
  blocking collectives: 154 us -> 0 us
  waiting for transfers between devices: 149 us -> 0 us
  Pallas kernels: 0 us -> 74.4 us
  between operations: 14.2 us -> 0.64 us
  matrix products: 6.85 us -> 0 us
  starting transfers between devices: 5.36 us -> 0 us
  other arithmetic: 4.61 us -> 0 us
    all_to_all x2 -> x0, blocking collectives: 154 us -> none  [the longest x1 116 us: from_everyone(): return lax.all_to_all(copies, axis, split_axis=0, concat_axis=0, tiled=True)]
    all_gather x1 -> x0, waiting for transfers between devices: 143 us -> none  [local(): lax.all_gather(projector, 'dp', axis=0, tiled=True)]
    pallas_call x0 -> x1, Pallas kernels: none -> 74.4 us  [local(): pl.pallas_call(functools.partial(kernel, scale), out_shape=(jax.ShapeDtyp...]
    dot_general x4 -> x0, matrix products: 6.85 us -> none  [the longest x1 4.63 us: local(): jnp.dot(activations, lax.all_gather(projector, 'dp', axis=0, tiled=True),...]
    ppermute x2 -> x0, waiting for transfers between devices: 5.68 us -> none  [from_behind(): return lax.ppermute(block, axis, route)]
    ppermute x2 -> x0, starting transfers between devices: 5.32 us -> none  [from_behind(): return lax.ppermute(block, axis, route)]
  transfers between devices with their start and end apart: 3 -> 0, of which waited for: 2 -> 0; matrix products, arithmetic and copies ran while one was open for 3% -> 0% of each run, Pallas kernels for 0% -> 0%
where the time goes in v1:
time: 78.3 us; the launch traced here: 78.1 us
  Pallas kernels  74.4 us (95%)
  local copies, waits for them, and re-layouts  3.04 us (4%)
    pallas_call x1, Pallas kernels, local(): pl.pallas_call(functools.partial(kernel, scale), out_shape=(jax.ShapeDtyp...  74.4 us
    unnamed x2, local copies, waits for them, and re-layouts  3.04 us

profile of v1, /device:TPU:1, one launch (start us, length us, event | category | flops | bytes accessed | tf_op | source)
XLA Modules:
  0.0 78.1 jit_solution(14149984277333340676)
XLA Ops:
  0.6 74.4 %shard_map.77 = (bf16[128,512]{1,0:T(8,128)(2,1)}, f32[32,512]{1,0:T(8,128)}) custom-call(bf16[128,8192]{1,0:T(8,128)(2,1)} %act_hbm.1, bf16[128,4096]{1,0:T(8,128)(2,1)} %q_hbm.1, bf16[128,512]{1,0:T(8,128)(2,1)} %k_hbm.1, bf16[128,4096]{1,0:T(8,128)(2,1)} %og_hbm.1, bf16[512,512]{1,0:T(8,128)(2,1)} %p_hbm.1, s32[1,96]{1,0:T(1,128)} %len_ref.1), custom_call_target="tpu_custom_call" | custom-call | tf_op jit(solution)/shard_map/pallas_call | solution.py:445
  75.0 1.6 %copy.10 = bf16[128,512]{1,0:T(8,128)(2,1)} copy(bf16[128,512]{1,0:T(8,128)(2,1)} %get-tuple-element.4) | data formatting | bytes 262144
  76.6 1.5 %copy.11 = f32[32,512]{1,0:T(8,128)} copy(f32[32,512]{1,0:T(8,128)} %get-tuple-element.5) | data formatting | bytes 131072

commit v2 on v1

v2 whole, which is shorter than its diff:
```python
import functools
import math

import jax
import jax.numpy as jnp
from jax import lax
from jax.experimental import pallas as pl
from jax.experimental.pallas import tpu as pltpu
from jax.sharding import PartitionSpec as P

HEADS = 32
KV = 4
HD = 128
GROUP = HEADS // KV
MESH = pl.DeviceIdType.MESH

NX, NY, NH, NL = 4, 8, 2, 6
NZ = NH * NL
BF = jnp.bfloat16
F32 = jnp.float32
VMEM_BYTES = 54528 * 1024


def slot_of(k, o):
    return k * 2 + o


def kernel(
    scale,
    act_hbm, q_hbm, k_hbm, og_hbm, p_hbm, len_ref,
    vg_ref, grad_ref,
    q_v, og_v, kboth, a_all, p_all, terms, prev_send, prev_recv, v_all, acc,
    lhs, core_send, core_recv, x_keep, x_send, x_recv, y_keep, y_send, y_recv,
    z_send, z_recv, g_all,
    lsem, asem_s, asem_r, ksem, xsem_s, xsem_r, ysem_s, ysem_r, zsem_s, zfsem_s, zsem_r,
    ytok, ztok, psem, vsem, csem, rxs, rxr, rys, ryr, rzs, rzr, rgs, rgr,
):
    dp = lax.axis_index("dp")
    me = lax.axis_index("fsdp")
    x, half, core = dp // 4, (dp // 2) % 2, dp % 2
    y, lo = me % NY, me // NY
    z = half * NL + lo
    par = y % 2
    qa, qb = 2 * par, 2 * par + 1
    ma, mb = 2 - 2 * par, 3 - 2 * par

    def dev(xx, yy, zz, cc):
        return ((xx * 2 + zz // NL) * 2 + cc, (zz % NL) * NY + yy)

    def x_dev(k):
        return dev((x + k) % NX, y, z, core)

    def y_dev(k):
        return dev(x, (y + k) % NY, z, core)

    def z_dev(k):
        return dev(x, y, (z + k) % NZ, core)

    mate = dev(x, y, z, 1 - core)
    has_prev, has_next = me > 0, me < NY * NL - 1

    def remote(src, dst, ssem, rsem, to):
        return pltpu.make_async_remote_copy(
            src_ref=src, dst_ref=dst, send_sem=ssem, recv_sem=rsem, device_id=to, device_id_type=MESH
        )

    def a_cols(k, o, cc):
        blk = (((x + k) % NX) * 2 + (half + o) % 2) * 2 + cc
        return pl.ds(pl.multiple_of(blk * 512, 512), 512)

    loads = [
        pltpu.make_async_copy(k_hbm, kboth.at[pl.ds(128, 128)], lsem.at[0]),
        pltpu.make_async_copy(q_hbm, q_v, lsem.at[1]),
        pltpu.make_async_copy(og_hbm, og_v, lsem.at[2]),
        pltpu.make_async_copy(p_hbm, p_all.at[0], lsem.at[3]),
    ]
    a_loads = [
        pltpu.make_async_copy(
            act_hbm.at[:, a_cols(s // 2, s % 2, core)], a_all.at[s, pl.ds(0, 128)], lsem.at[4 + s]
        )
        for s in range(8)
    ]
    for c in loads:
        c.start()

    barrier = pltpu.get_barrier_semaphore()
    peers = [mate, x_dev(1), x_dev(-1), x_dev(2), y_dev(1), y_dev(-1), z_dev(1), z_dev(-1)]
    for to in peers:
        pl.semaphore_signal(barrier, inc=1, device_id=to, device_id_type=MESH)
    cross_next = jnp.logical_and(y == NY - 1, lo < NL - 1)
    cross_prev = jnp.logical_and(y == 0, lo > 0)

    @pl.when(cross_next)
    def _():
        pl.semaphore_signal(barrier, inc=1, device_id=(dp, me + 1), device_id_type=MESH)

    @pl.when(cross_prev)
    def _():
        pl.semaphore_signal(barrier, inc=1, device_id=(dp, me - 1), device_id_type=MESH)

    for c in a_loads:
        c.start()

    n_docs = len_ref.shape[1]
    lens = jnp.broadcast_to(len_ref[...].astype(F32), (128, n_docs)).astype(BF)
    upto = (
        lax.broadcasted_iota(jnp.int32, (n_docs, n_docs), 1)
        <= lax.broadcasted_iota(jnp.int32, (n_docs, n_docs), 0)
    )
    ends = lax.dot_general(
        jnp.where(upto, 1.0, 0.0).astype(BF), lens, (((1,), (1,)), ((), ())), preferred_element_type=F32
    ).astype(jnp.int32)
    q_pos = me * 128 + lax.broadcasted_iota(jnp.int32, (n_docs, 128), 1)
    start = jnp.max(jnp.where(ends <= q_pos, ends, 0), axis=0, keepdims=True)
    key_pos = (me - 1) * 128 + lax.broadcasted_iota(jnp.int32, (256, 128), 0)
    qry_pos = me * 128 + lax.broadcasted_iota(jnp.int32, (256, 128), 1)
    visible = jnp.logical_and(
        jnp.logical_and(key_pos >= start, key_pos <= qry_pos), key_pos >= 0
    )
    visible2 = jnp.concatenate([visible, visible], axis=1)

    @pl.when(jnp.logical_not(has_prev))
    def _():
        kboth[pl.ds(0, 128), :] = jnp.zeros((128, KV * HD), BF)

    @pl.when(jnp.logical_not(has_next))
    def _():
        prev_recv[...] = jnp.zeros((128, KV * HD), BF)

    pl.semaphore_wait(
        barrier, len(peers) + cross_next.astype(jnp.int32) + cross_prev.astype(jnp.int32)
    )

    def tokens(axis, r):
        sems, to = ((ytok, y_dev), (ztok, z_dev))[axis]
        return [(sems.at[r, 0], to(1)), (sems.at[r, 1], to(-1))]

    rounds = (NY // 2 - 1, NZ // 2 - 1)

    def token_send(r):
        for axis in range(2):
            if r < rounds[axis]:
                for sem, to in tokens(axis, r):
                    pl.semaphore_signal(sem, inc=1, device_id=to, device_id_type=MESH)

    def token_step(r):
        for axis in range(2):
            if r < rounds[axis]:
                for sem, _ in tokens(axis, r):
                    pl.semaphore_wait(sem, 1)
        token_send(r + 1)

    token_send(0)

    k_copy = remote(k_hbm, kboth.at[pl.ds(0, 128)], ksem.at[0], ksem.at[1], (dp, me + 1))

    @pl.when(has_next)
    def _():
        k_copy.start()

    def rows_of(e):
        side = par if e < 4 else 1 - par
        return pl.ds(pl.multiple_of(side * 256 + e % 4 * 64, 64), 64)

    def p_part(s, e):
        return p_all.at[s, rows_of(e)]

    def x_copy(o, d, e):
        src = p_hbm.at[rows_of(e)] if o == 0 else p_part(slot_of(0, 1), e)
        return remote(
            src,
            p_part(slot_of((3, 1, 2)[d], o), e),
            xsem_s.at[o, d, e],
            xsem_r.at[o, d, e],
            x_dev((1, -1, 2)[d]),
        )

    def y_copy(s, e):
        return remote(
            p_part(s, e), p_part(s, e), ysem_s.at[s, e], ysem_r.at[s, e], y_dev(-1 if e % 2 else 1)
        )

    def y_wait(s):
        for e in range(4):
            remote(
                p_part(s, e + 4), p_part(s, e + 4), ysem_s.at[s, e], ysem_r.at[s, e],
                y_dev(-1 if e % 2 else 1),
            ).wait_recv()

    low_side = lo < 3
    z_away = jnp.where(low_side, 1, NZ - 1)
    z_out = jnp.where(lo == 0, NZ - 1, 1)
    z_edge = jnp.logical_or(lo == 0, lo == NL - 1)
    z_mid = jnp.logical_or(lo == 2, lo == 3)
    z_second = jnp.logical_or(lo == 1, lo == 4)

    def z_own(e):
        return remote(
            p_hbm.at[rows_of(e)], p_part(1, e), zsem_s.at[e], zsem_r.at[e],
            dev(x, y, (z + z_out) % NZ, core),
        )

    def z_on(e):
        return remote(
            p_part(1, e), p_part(1, e), zfsem_s.at[e], zsem_r.at[e],
            dev(x, y, (z + z_away) % NZ, core),
        )

    @pl.when(z_edge)
    def _():
        for e in range(4):
            z_own(e).start()

    for e in range(4):
        for d in range(3):
            x_copy(0, d, e).start()

    @pl.when(z_edge)
    def _():
        for e in range(4, 8):
            z_own(e).start()

    a_copies = [
        remote(
            act_hbm.at[:, a_cols(s // 2, s % 2, 1 - core)],
            a_all.at[s, pl.ds(128, 128)],
            asem_s.at[s],
            asem_r.at[s],
            mate,
        )
        for s in range(8)
    ]
    for c in a_copies:
        c.start()

    def z_step(kind, chunks):
        @pl.when(kind)
        def _():
            for e in chunks:
                z_copy = z_on(e)
                z_copy.wait_recv()
                if kind is not z_mid:
                    z_copy.start()
                if e < 4:
                    for d in (2, 0, 1):
                        x_copy(1, d, e).start()

    def x_step(o, e):
        for d in (0, 1, 2):
            x_copy(o, d, e).wait_recv()
            y_copy(slot_of((3, 1, 2)[d], o), e).start()

    factor = math.log2(math.e) / math.sqrt(HD)

    def attend(g):
        keys = kboth[:, g * HD : (g + 1) * HD]
        total = jnp.zeros((256, HD), F32)
        for pair in range(GROUP // 2):
            h0 = (g * GROUP + 2 * pair) * HD
            qs = jnp.concatenate([q_v[:, h0 : h0 + HD], q_v[:, h0 + HD : h0 + 2 * HD]], axis=0)
            gs = jnp.concatenate([og_v[:, h0 : h0 + HD], og_v[:, h0 + HD : h0 + 2 * HD]], axis=0)
            s = lax.dot_general(keys, qs, (((1,), (1,)), ((), ())), preferred_element_type=F32)
            s = jnp.where(visible2, s, -jnp.inf)
            e = jnp.exp2((s - jnp.max(s, axis=0, keepdims=True)) * factor)
            w = (e * (1.0 / jnp.sum(e, axis=0, keepdims=True))).astype(BF)
            total = total + jnp.dot(w, gs, preferred_element_type=F32)
        terms[:, g * HD : (g + 1) * HD] = total[128:]
        prev_send[:, g * HD : (g + 1) * HD] = total[:128].astype(BF)

    for c in loads[:3]:
        c.wait()
    z_step(z_edge, (0,))
    x_step(0, 0)
    z_step(z_edge, (1,))

    @pl.when(has_prev)
    def _():
        k_copy.wait_recv()

    attend(0)
    z_step(z_edge, (2, 3))
    z_step(z_second, (0,))
    x_step(0, 1)
    attend(1)
    z_step(z_second, (1, 2))
    x_step(0, 2)
    z_step(z_edge, (4, 5))
    attend(2)
    z_step(z_second, (3,))
    z_step(z_mid, (0,))
    x_step(0, 3)
    attend(3)
    prev_copy = remote(prev_send, prev_recv, psem.at[0], psem.at[1], (dp, me - 1))

    @pl.when(has_prev)
    def _():
        prev_copy.start()

    z_step(z_edge, (6, 7))
    z_step(z_mid, (1, 2))
    z_step(z_second, (4, 5))
    z_step(z_mid, (3,))
    z_step(z_second, (6, 7))
    x_step(1, 0)

    loads[3].wait()
    for c in a_loads:
        c.wait()
    for c in a_copies:
        c.wait_recv()

    def project(s):
        return jnp.dot(a_all[s], p_all[s], preferred_element_type=F32)

    acc[...] = project(0)
    token_step(0)
    x_step(1, 1)
    token_step(1)

    @pl.when(has_next)
    def _():
        prev_copy.wait_recv()

    grads = (terms[...] + prev_recv[...].astype(F32)).astype(BF)
    vg_ref[...] = grads
    v_all[pl.ds(0, 128), :] = grads
    v_copy = remote(
        v_all.at[pl.ds(0, 128)], v_all.at[pl.ds(128, 128)], vsem.at[0], vsem.at[1], mate
    )
    v_copy.start()
    x_step(1, 2)
    token_step(2)
    x_step(1, 3)
    token_step(3)
    token_step(4)
    for s in (slot_of(3, 0), slot_of(1, 0), slot_of(2, 0)):
        y_wait(s)
        acc[...] += project(s)
    z_step(z_mid, (4, 5, 6, 7))
    acc[...] += project(slot_of(0, 1))
    for s in (slot_of(3, 1), slot_of(1, 1), slot_of(2, 1)):
        y_wait(s)
        acc[...] += project(s)

    flipped = acc[...].T
    high = flipped.astype(BF)
    low = (flipped - high.astype(F32)).astype(BF)
    for b in range(16):
        at = (b % 2, b // 2 % 2, slice(b // 4 * 32, b // 4 * 32 + 32))
        lhs[at + (slice(0, 256),)] = high[b * 32 : b * 32 + 32]
        lhs[at + (slice(256, 512),)] = low[b * 32 : b * 32 + 32]
    v_copy.wait_recv()
    values = jnp.concatenate([v_all[...], v_all[...]], axis=0)

    halves = (1 - half, half)

    def term(cc, hh):
        return jnp.dot(lhs[cc, hh], values, preferred_element_type=F32) * scale

    rc = [
        remote(core_send.at[t], core_recv.at[t], csem.at[0, t], csem.at[1, t], mate)
        for t in range(2)
    ]
    for t in range(2):
        core_send[t] = term(1 - core, halves[t]).astype(BF)
        rc[t].start()
    rx = [
        [
            remote(
                x_send.at[t, (x + k) % NX], x_recv.at[t, k - 1], rxs.at[t, k - 1], rxr.at[t, k - 1],
                x_dev(k),
            )
            for k in range(1, NX)
        ]
        for t in range(2)
    ]
    ry = [
        [
            remote(
                y_send.at[t, (y + k) % NY], y_recv.at[t, k - 1], rys.at[t, k - 1], ryr.at[t, k - 1],
                y_dev(k),
            )
            for k in range(1, NY)
        ]
        for t in range(2)
    ]
    rz_far = [
        remote(
            z_send.at[0], z_recv.at[k], rzs.at[k], rzr.at[k],
            dev(x, y, (1 - half) * NL + (lo + k) % NL, core),
        )
        for k in range(NL)
    ]
    rz_near = [
        remote(
            z_send.at[1], z_recv.at[NL + k - 1], rzs.at[NL + k - 1], rzr.at[NL + k - 1],
            dev(x, y, half * NL + (lo + k) % NL, core),
        )
        for k in range(1, NL)
    ]
    for t in range(2):
        mine = term(core, halves[t])
        rc[t].wait_recv()
        mine = (mine + core_recv[t].astype(F32)).reshape(NX, 32, 512)
        x_keep[t] = mine
        x_send[t] = mine.astype(BF)
        for k in (2, 1, 3):
            rx[t][k - 1].start()
    for t in range(2):
        mine = x_keep[t, x]
        for k in (1, 3, 2):
            rx[t][k - 1].wait_recv()
            mine = mine + x_recv[t, k - 1].astype(F32)
        for yy in range(NY):
            piece = mine[yy // 4 * 16 : yy // 4 * 16 + 16, yy % 4 * 128 : yy % 4 * 128 + 128]
            y_keep[t, yy] = piece
            y_send[t, yy] = piece.astype(BF)
        for k in (4, 3, 5, 2, 6, 1, 7):
            ry[t][k - 1].start()
    for t in range(2):
        mine = y_keep[t, y]
        for k in (1, 7, 2, 6, 3, 5, 4):
            ry[t][k - 1].wait_recv()
            mine = mine + y_recv[t, k - 1].astype(F32)
        z_send[t] = mine.astype(BF)
        for c in (rz_far, rz_near)[t]:
            c.start()
    for k, c in enumerate(rz_near):
        c.wait_recv()
        mine = mine + z_recv[NL + k].astype(F32)
    for k, c in enumerate(rz_far):
        c.wait_recv()
        mine = mine + z_recv[k].astype(F32)
    g_all[y] = mine
    rg = [
        remote(g_all.at[y], g_all.at[y], rgs.at[k - 1], rgr.at[k - 1], y_dev(k)) for k in range(1, NY)
    ]
    for k in (4, 3, 5, 2, 6, 1, 7):
        rg[k - 1].start()
    for k in range(1, NY):
        sender = (y + NY - k) % NY
        remote(
            g_all.at[sender], g_all.at[sender], rgs.at[k - 1], rgr.at[k - 1], y_dev(k)
        ).wait_recv()
    for yy in range(NY):
        grad_ref[pl.ds(yy // 4 * 16, 16), pl.ds(yy % 4 * 128, 128)] = g_all[yy]

    @pl.when(has_next)
    def _():
        k_copy.wait_send()

    @pl.when(has_prev)
    def _():
        prev_copy.wait_send()

    @pl.when(z_edge)
    def _():
        for e in range(8):
            z_own(e).wait_send()

    @pl.when(jnp.logical_not(z_mid))
    def _():
        for e in range(8):
            z_on(e).wait_send()

    for o in range(2):
        for e in range(4):
            for d in range(3):
                x_copy(o, d, e).wait_send()
    for s in range(2, 8):
        for e in range(4):
            y_copy(s, e).wait_send()
    for c in a_copies + [v_copy] + rc + rx[0] + rx[1] + ry[0] + ry[1] + rz_far + rz_near + rg:
        c.wait_send()


def local(activations, queries, key_states, out_grads, projector, lengths):
    toks = queries.shape[0]
    scale = 1.0 / math.sqrt(toks * lax.axis_size("dp") * lax.axis_size("fsdp"))
    dma, vmem = pltpu.SemaphoreType.DMA, pltpu.VMEM
    any_spec = pl.BlockSpec(memory_space=pltpu.HBM)
    vmem_spec = pl.BlockSpec(memory_space=pltpu.VMEM)
    return pl.pallas_call(
        functools.partial(kernel, scale),
        out_shape=(
            jax.ShapeDtypeStruct((toks, KV * HD), BF),
            jax.ShapeDtypeStruct((32, KV * HD), F32),
        ),
        in_specs=[any_spec] * 5 + [vmem_spec],
        out_specs=(vmem_spec, vmem_spec),
        scratch_shapes=[
            vmem((toks, HEADS * HD), BF),
            vmem((toks, HEADS * HD), BF),
            vmem((2 * toks, KV * HD), BF),
            vmem((8, 2 * toks, 512), BF),
            vmem((8, 512, 512), BF),
            vmem((toks, KV * HD), F32),
            vmem((toks, KV * HD), BF),
            vmem((toks, KV * HD), BF),
            vmem((2 * toks, KV * HD), BF),
            vmem((2 * toks, 512), F32),
            vmem((2, NH, 128, 512), BF),
            vmem((2, 128, 512), BF),
            vmem((2, 128, 512), BF),
            vmem((2, NX, 32, 512), F32),
            vmem((2, NX, 32, 512), BF),
            vmem((2, NX - 1, 32, 512), BF),
            vmem((2, NY, 16, 128), F32),
            vmem((2, NY, 16, 128), BF),
            vmem((2, NY - 1, 16, 128), BF),
            vmem((2, 16, 128), BF),
            vmem((NZ - 1, 16, 128), BF),
            vmem((NY, 16, 128), F32),
            dma((12,)),
            dma((8,)),
            dma((8,)),
            dma((2,)),
            dma((2, 3, 4)),
            dma((2, 3, 4)),
            dma((8, 4)),
            dma((8, 4)),
            dma((8,)),
            dma((8,)),
            dma((8,)),
            pltpu.SemaphoreType.REGULAR((NY // 2 - 1, 2)),
            pltpu.SemaphoreType.REGULAR((NZ // 2 - 1, 2)),
            dma((2,)),
            dma((2,)),
            dma((2, 2)),
            dma((2, NX - 1)),
            dma((2, NX - 1)),
            dma((2, NY - 1)),
            dma((2, NY - 1)),
            dma((NZ - 1,)),
            dma((NZ - 1,)),
            dma((NY - 1,)),
            dma((NY - 1,)),
        ],
        compiler_params=pltpu.CompilerParams(
            collective_id=0, has_side_effects=True, vmem_limit_bytes=VMEM_BYTES
        ),
    )(activations, queries, key_states, out_grads, projector, lengths)


def solution(mesh):
    in_specs = (
        P(("dp", "fsdp"), None),
        P(("dp", "fsdp"), None),
        P(("dp", "fsdp"), None),
        P(("dp", "fsdp"), None),
        P("dp", None),
        P("dp", None),
    )
    out_specs = (P(("dp", "fsdp"), None), P("dp", None))
    return jax.shard_map(local, mesh=mesh, in_specs=in_specs, out_specs=out_specs, check_vma=False)
```

time: 78.3 us -> 72.8 us (0.930)
  Pallas kernels: 74.4 us -> 69 us
    pallas_call x1, Pallas kernels: 74.4 us -> 69 us  [local(): pl.pallas_call(functools.partial(kernel, scale), out_shape=(jax.ShapeDtyp...]
    unnamed x2 -> x6, local copies, waits for them, and re-layouts: 3.04 us -> 2.84 us
where the time goes in v2:
time: 72.8 us; the launch traced here: 72.5 us
  Pallas kernels  69 us (95%)
  local copies, waits for them, and re-layouts  2.84 us (4%)
    pallas_call x1, Pallas kernels, local(): pl.pallas_call(functools.partial(kernel, scale), out_shape=(jax.ShapeDtyp...  69 us
    unnamed x6, local copies, waits for them, and re-layouts  2.84 us

profile of v2, /device:TPU:1, one launch (start us, length us, event | category | flops | bytes accessed | tf_op | source)
XLA Modules:
  0.0 72.5 jit_solution(8553172835699788697)
XLA Ops:
  0.6 0.0 copy-start
  0.6 0.9 %copy-done = bf16[128,512]{1,0:T(8,128)(2,1)S(1)} copy-done((bf16[128,512]{1,0:T(8,128)(2,1)S(1)}, bf16[128,512]{1,0:T(8,128)(2,1)}, u32[]{:S(2)}) %copy-start) | copy-done | bytes 131096
  1.5 0.0 copy-start.1
  1.5 0.7 copy-done.1
  2.2 69.0 %shard_map.77 = (bf16[128,512]{1,0:T(8,128)(2,1)S(1)}, f32[32,512]{1,0:T(8,128)S(1)}) custom-call(bf16[128,8192]{1,0:T(8,128)(2,1)} %act_hbm.1, bf16[128,4096]{1,0:T(8,128)(2,1)} %q_hbm.1, bf16[128,512]{1,0:T(8,128)(2,1)S(1)} %copy-done, bf16[128,4096]{1,0:T(8,128)(2,1)} %og_hbm.1, bf16[512,512]{1,0:T(8,128)(2,1)} %p_hbm.1, s32[1,96]{1,0:T(1,128)S(1)} %copy-done.1), custom_call_target="tpu_custom_call" | custom-call | tf_op jit(solution)/shard_map/pallas_call | solution.py:483
  71.2 0.7 copy.10
  71.9 0.6 copy.11
Async XLA Ops:
  0.6 0.9 %copy-start = (bf16[128,512]{1,0:T(8,128)(2,1)S(1)}, bf16[128,512]{1,0:T(8,128)(2,1)}, u32[]{:S(2)}) copy-start(bf16[128,512]{1,0:T(8,128)(2,1)} %k_hbm.1) | copy-start | bytes 393220
  1.5 0.7 copy-start.1
